TPU v7x, 32 devices: a whole 2x2x4 slice. The times are simulated.
32 devices in a mesh: energy: 4 (over y, x), slab: 8 (over z, core).
Axes of the slice: x: 2, y: 2, z: 4, core: 2. Of those that a mesh axis runs over, the one named last changes fastest.
Arguments:
- green_init: float32 [32, 8, 2, 128, 128], P('energy', 'slab'), may hold values from -6 to 6
- retarded: float32 [32, 8, 2, 128, 128], P('energy', 'slab'), may hold values from -0.25 to 0.25
- coupling_on: float32 [8, 128, 128], P('slab'), may hold values from -0.5 to 0.5
- coupling_lower: float32 [8, 128, 128], P('slab'), may hold values from -0.5 to 0.5
- coupling_upper: float32 [8, 128, 128], P('slab'), may hold values from -0.5 to 0.5
- phonon_weights: float32 [4], replicated, may hold values from 0.3 to 1
Outputs:
- green_final: float32 [32, 8, 2, 128, 128], P('energy', 'slab')
All inputs are finite; a program needn't handle non-finite values.
Results may differ from a plain program's by a relative error of at most 0.0001.
Values sent between devices are 32-bit elements; how exact they have to be, the bound alone decides.
A program may use at most 64 MiB of HBM per device.

v0:
```python
import jax
import jax.numpy as jnp
from jax import lax
from jax.sharding import PartitionSpec as P

SHIFT_NEAR = 3
SHIFT_FAR = 7
ITERS = 2


HIGH = lax.Precision.HIGHEST


def with_halo(cells, sides, width):
    for axis, dim in sides:
        count = lax.axis_size(axis)
        ends = count - 1
        head = lax.slice_in_dim(cells, 0, width, axis=dim)
        tail = lax.slice_in_dim(cells, cells.shape[dim] - width, cells.shape[dim], axis=dim)
        cells = jnp.concatenate(
            [
                lax.ppermute(tail, axis, [(i, (i + 1) % count) for i in range(ends)]),
                cells,
                lax.ppermute(head, axis, [((i + 1) % count, i) for i in range(ends)]),
            ],
            axis=dim,
        )
    return cells


def sandwich(coupling, values):
    half_done = jnp.einsum("ij,ecjk->ecik", coupling, values, precision=HIGH)
    return jnp.einsum("ecik,lk->ecil", half_done, coupling, precision=HIGH)


def matmul_plain(left, right):
    return jnp.einsum("eij,ejk->eik", left, right, precision=HIGH)


def matmul_adjoint(left, right):
    return jnp.einsum("eij,ekj->eik", left, right, precision=HIGH)


def propagate(ret_block, self_energy):
    ret_re, ret_im = (ret_block[:, 0], ret_block[:, 1])
    sig_re, sig_im = (self_energy[:, 0], self_energy[:, 1])
    prod_re = matmul_plain(ret_re, sig_re) - matmul_plain(ret_im, sig_im)
    prod_im = matmul_plain(ret_re, sig_im) + matmul_plain(ret_im, sig_re)
    out_re = matmul_adjoint(prod_re, ret_re) + matmul_adjoint(prod_im, ret_im)
    out_im = matmul_adjoint(prod_im, ret_re) - matmul_adjoint(prod_re, ret_im)
    return jnp.stack([out_re, out_im], 1)


def local(green_init, retarded, coupling_on, coupling_lower, coupling_upper, phonon_weights):
    current = green_init[:, 0]
    local_ret = retarded[:, 0]
    energies = current.shape[0]
    for born_step in range(ITERS):
        wider = with_halo(current, (("energy", 0),), SHIFT_FAR)
        lower_far = wider[0:energies]
        lower_near = wider[SHIFT_FAR - SHIFT_NEAR : SHIFT_FAR - SHIFT_NEAR + energies]
        upper_near = wider[SHIFT_FAR + SHIFT_NEAR : SHIFT_FAR + SHIFT_NEAR + energies]
        upper_far = wider[2 * SHIFT_FAR : 2 * SHIFT_FAR + energies]
        mixture = phonon_weights[0] * upper_far
        mixture = mixture + phonon_weights[1] * upper_near
        mixture = mixture + phonon_weights[2] * lower_near
        mixture = mixture + phonon_weights[3] * lower_far
        slab_rim = with_halo(mixture[:, None], (("slab", 1),), 1)
        self_energy = sandwich(coupling_on[0], slab_rim[:, 1])
        self_energy = self_energy + sandwich(coupling_lower[0], slab_rim[:, 0])
        self_energy = self_energy + sandwich(coupling_upper[0], slab_rim[:, 2])
        current = propagate(local_ret, self_energy)
    return current[:, None]


def solution(mesh):
    in_specs = (
        P("energy", "slab", None, None, None),
        P("energy", "slab", None, None, None),
        P("slab", None, None),
        P("slab", None, None),
        P("slab", None, None),
        P(),
    )
    out_specs = P("energy", "slab", None, None, None)
    return jax.shard_map(local, mesh=mesh, in_specs=in_specs, out_specs=out_specs, check_vma=False)
```

profile of v0, /device:TPU:5, one launch (start us, length us, event | category | flops | bytes accessed | tf_op | source)
XLA Modules:
  0.0 153.2 jit_solution(9311274671293487539)
XLA Ops:
  0.0 1.3 copy.69
  1.6 3.1 %collective-permute-start = (f32[7,2,128,128]{3,2,0,1:T(8,128)S(1)}, f32[7,2,128,128]{3,2,0,1:T(8,128)S(1)}, u32[]{:S(2)}, u32[]{:S(2)}) collective-permute-start(f32[7,2,128,128]{3,2,0,1:T(8,128)S(1)} %get-tuple-element.9), channel_id=1, source_target_pairs={{8,0},{16,8},{24,16},{9,1},{17,9},{25,17},{10,2},{18,10},{26,18},{... | collective-permute-start | bytes 2752520 | tf_op jit(solution)/shard_map/ppermute | solution.py:24
  4.6 2.3 %collective-permute-start.1 = (f32[7,2,128,128]{3,2,0,1:T(8,128)S(1)}, f32[7,2,128,128]{3,2,0,1:T(8,128)S(1)}, u32[]{:S(2)}, u32[]{:S(2)}) collective-permute-start(f32[7,2,128,128]{3,2,0,1:T(8,128)S(1)} %get-tuple-element.10), channel_id=1, source_target_pairs={{0,8},{8,16},{16,24},{1,9},{9,17},{17,25},{2,10},{10,18},{18,26},{... | collective-permute-start | bytes 2752520 | tf_op jit(solution)/shard_map/ppermute | solution.py:22
  7.6 17.1 %collective-permute-done = f32[7,2,128,128]{3,2,0,1:T(8,128)S(1)} collective-permute-done((f32[7,2,128,128]{3,2,0,1:T(8,128)S(1)}, f32[7,2,128,128]{3,2,0,1:T(8,128)S(1)}, u32[]{:S(2)}, u32[]{:S(2)}) %collective-permute-start) | collective-permute-done | bytes 917536 | tf_op jit(solution)/shard_map/ppermute | solution.py:24
  24.7 19.6 %collective-permute-done.1 = f32[7,2,128,128]{3,2,0,1:T(8,128)S(1)} collective-permute-done((f32[7,2,128,128]{3,2,0,1:T(8,128)S(1)}, f32[7,2,128,128]{3,2,0,1:T(8,128)S(1)}, u32[]{:S(2)}, u32[]{:S(2)}) %collective-permute-start.1) | collective-permute-done | bytes 917536 | tf_op jit(solution)/shard_map/ppermute | solution.py:22
  44.3 2.9 %fusion.7 = f32[8,2,128,128]{3,2,0,1:T(8,128)S(1)} fusion(f32[7,2,128,128]{3,2,0,1:T(8,128)S(1)} %collective-permute-done.1, f32[8,2,128,128]{3,2,0,1:T(8,128)S(1)} %bitcast.159, f32[7,2,128,128]{3,2,0,1:T(8,128)S(1)} %collective-permute-done, f32[]{:T(128)} %bitcast.6, f32[]{:T(128)} %bitcast.4, f32[]{:T(128)} %bitcast.3, f32[]{:T(128)} %bitcast), kind=kLoop, calls=%fused_computation.31 | loop fusion | flops 2883584 | bytes 3932176 | tf_op jit(solution)/shard_map/add | solution.py:67
  47.2 4.6 %collective-permute-start.2 = (f32[8,1,2,128,128]{4,3,0,2,1:T(8,128)S(1)}, f32[8,1,2,128,128]{4,3,0,2,1:T(8,128)S(1)}, u32[]{:S(2)}, u32[]{:S(2)}) collective-permute-start(f32[8,1,2,128,128]{4,3,0,2,1:T(8,128)S(1)} %bitcast.162), channel_id=1, source_target_pairs={{0,1},{1,2},{2,3},{3,4},{4,5},{5,6},{6,7},{8,9},{9,10},{10,11},{11... | collective-permute-start | bytes 3145736 | tf_op jit(solution)/shard_map/ppermute | solution.py:22
  51.9 2.1 %collective-permute-start.3 = (f32[8,1,2,128,128]{4,3,0,2,1:T(8,128)S(1)}, f32[8,1,2,128,128]{4,3,0,2,1:T(8,128)S(1)}, u32[]{:S(2)}, u32[]{:S(2)}) collective-permute-start(f32[8,1,2,128,128]{4,3,0,2,1:T(8,128)S(1)} %bitcast.163), channel_id=1, source_target_pairs={{1,0},{2,1},{3,2},{4,3},{5,4},{6,5},{7,6},{9,8},{10,9},{11,10},{12... | collective-permute-start | bytes 3145736 | tf_op jit(solution)/shard_map/ppermute | solution.py:24
  54.0 1.1 convolution_bitcast_fusion.5
  56.1 7.5 %collective-permute-done.2 = f32[8,1,2,128,128]{4,3,0,2,1:T(8,128)S(1)} collective-permute-done((f32[8,1,2,128,128]{4,3,0,2,1:T(8,128)S(1)}, f32[8,1,2,128,128]{4,3,0,2,1:T(8,128)S(1)}, u32[]{:S(2)}, u32[]{:S(2)}) %collective-permute-start.2) | collective-permute-done | bytes 1048608 | tf_op jit(solution)/shard_map/ppermute | solution.py:22
  63.6 1.1 convolution_bitcast_fusion.4
  65.6 2.5 %collective-permute-done.3 = f32[8,1,2,128,128]{4,3,0,2,1:T(8,128)S(1)} collective-permute-done((f32[8,1,2,128,128]{4,3,0,2,1:T(8,128)S(1)}, f32[8,1,2,128,128]{4,3,0,2,1:T(8,128)S(1)}, u32[]{:S(2)}, u32[]{:S(2)}) %collective-permute-start.3) | collective-permute-done | bytes 1048608 | tf_op jit(solution)/shard_map/ppermute | solution.py:24
  68.2 1.1 convolution_bitcast_fusion.3
  72.3 1.0 convolution_add_fusion.7
  74.4 1.0 convolution_subtract_fusion.3
  75.4 1.2 fusion.30
  78.9 1.9 %collective-permute-start.4 = (f32[7,2,128,128]{3,2,0,1:T(8,128)S(1)}, f32[7,2,128,128]{3,2,0,1:T(8,128)S(1)}, u32[]{:S(2)}, u32[]{:S(2)}) collective-permute-start(f32[7,2,128,128]{3,2,0,1:T(8,128)S(1)} %get-tuple-element.7), channel_id=1, source_target_pairs={{8,0},{16,8},{24,16},{9,1},{17,9},{25,17},{10,2},{18,10},{26,18},{... | collective-permute-start | bytes 2752520 | tf_op jit(solution)/shard_map/ppermute | solution.py:24
  80.9 3.4 %collective-permute-start.5 = (f32[7,2,128,128]{3,2,0,1:T(8,128)S(1)}, f32[7,2,128,128]{3,2,0,1:T(8,128)S(1)}, u32[]{:S(2)}, u32[]{:S(2)}) collective-permute-start(f32[7,2,128,128]{3,2,0,1:T(8,128)S(1)} %get-tuple-element.8), channel_id=1, source_target_pairs={{0,8},{8,16},{16,24},{1,9},{9,17},{17,25},{2,10},{10,18},{18,26},{... | collective-permute-start | bytes 2752520 | tf_op jit(solution)/shard_map/ppermute | solution.py:22
  84.3 15.2 %collective-permute-done.4 = f32[7,2,128,128]{3,2,0,1:T(8,128)S(1)} collective-permute-done((f32[7,2,128,128]{3,2,0,1:T(8,128)S(1)}, f32[7,2,128,128]{3,2,0,1:T(8,128)S(1)}, u32[]{:S(2)}, u32[]{:S(2)}) %collective-permute-start.4) | collective-permute-done | bytes 917536 | tf_op jit(solution)/shard_map/ppermute | solution.py:24
  99.5 9.8 %collective-permute-done.5 = f32[7,2,128,128]{3,2,0,1:T(8,128)S(1)} collective-permute-done((f32[7,2,128,128]{3,2,0,1:T(8,128)S(1)}, f32[7,2,128,128]{3,2,0,1:T(8,128)S(1)}, u32[]{:S(2)}, u32[]{:S(2)}) %collective-permute-start.5) | collective-permute-done | bytes 917536 | tf_op jit(solution)/shard_map/ppermute | solution.py:22
  109.8 2.8 %fusion.11 = f32[8,2,128,128]{3,2,0,1:T(8,128)S(1)} fusion(f32[15,2,128,128]{3,2,0,1:T(8,128)S(1)} %get-tuple-element.6, f32[15,2,128,128]{3,2,0,1:T(8,128)S(1)} %get-tuple-element.5, f32[]{:T(128)} %bitcast.6, f32[]{:T(128)} %bitcast.4, f32[]{:T(128)} %bitcast.3, f32[]{:T(128)} %bitcast), kind=kLoop, calls=%fused_computation.36 | loop fusion | flops 1835008 | bytes 5242896 | tf_op jit(solution)/shard_map/add | solution.py:67
  112.6 12.8 %collective-permute-start.6 = (f32[8,1,2,128,128]{4,3,0,2,1:T(8,128)S(1)}, f32[8,1,2,128,128]{4,3,0,2,1:T(8,128)S(1)}, u32[]{:S(2)}, u32[]{:S(2)}) collective-permute-start(f32[8,1,2,128,128]{4,3,0,2,1:T(8,128)S(1)} %bitcast.160), channel_id=1, source_target_pairs={{0,1},{1,2},{2,3},{3,4},{4,5},{5,6},{6,7},{8,9},{9,10},{10,11},{11... | collective-permute-start | bytes 3145736 | tf_op jit(solution)/shard_map/ppermute | solution.py:22
  125.4 1.9 %collective-permute-start.7 = (f32[8,1,2,128,128]{4,3,0,2,1:T(8,128)S(1)}, f32[8,1,2,128,128]{4,3,0,2,1:T(8,128)S(1)}, u32[]{:S(2)}, u32[]{:S(2)}) collective-permute-start(f32[8,1,2,128,128]{4,3,0,2,1:T(8,128)S(1)} %bitcast.161), channel_id=1, source_target_pairs={{1,0},{2,1},{3,2},{4,3},{5,4},{6,5},{7,6},{9,8},{10,9},{11,10},{12... | collective-permute-start | bytes 3145736 | tf_op jit(solution)/shard_map/ppermute | solution.py:24
  127.3 1.1 convolution_bitcast_fusion.2
  129.4 7.7 %collective-permute-done.6 = f32[8,1,2,128,128]{4,3,0,2,1:T(8,128)S(1)} collective-permute-done((f32[8,1,2,128,128]{4,3,0,2,1:T(8,128)S(1)}, f32[8,1,2,128,128]{4,3,0,2,1:T(8,128)S(1)}, u32[]{:S(2)}, u32[]{:S(2)}) %collective-permute-start.6) | collective-permute-done | bytes 1048608 | tf_op jit(solution)/shard_map/ppermute | solution.py:22
  137.1 1.1 convolution_bitcast_fusion.1
  139.2 2.3 %collective-permute-done.7 = f32[8,1,2,128,128]{4,3,0,2,1:T(8,128)S(1)} collective-permute-done((f32[8,1,2,128,128]{4,3,0,2,1:T(8,128)S(1)}, f32[8,1,2,128,128]{4,3,0,2,1:T(8,128)S(1)}, u32[]{:S(2)}, u32[]{:S(2)}) %collective-permute-start.7) | collective-permute-done | bytes 1048608 | tf_op jit(solution)/shard_map/ppermute | solution.py:24
  141.5 1.1 convolution_bitcast_fusion
  145.6 1.0 convolution_add_fusion.5
  147.7 1.0 convolution_subtract_fusion.1
  148.7 1.3 fusion.28
  152.2 1.1 copy.27
  (32 shorter events, 18.0 us)
Async XLA Ops:
  0.0 54.0 %copy-start = (f32[1,128,128]{2,1,0:T(8,128)S(1)}, f32[1,128,128]{2,1,0:T(8,128)}, u32[]{:S(2)}) copy-start(f32[1,128,128]{2,1,0:T(8,128)} %param.8) | copy-start | bytes 196612
  1.4 5.6 %copy-start.4 = (f32[4]{0:T(128)S(1)}, f32[4]{0:T(128)}, u32[]{:S(2)}) copy-start(f32[4]{0:T(128)} %param.11) | copy-start | bytes 52
  1.6 23.1 %collective-permute-start = (f32[7,2,128,128]{3,2,0,1:T(8,128)S(1)}, f32[7,2,128,128]{3,2,0,1:T(8,128)S(1)}, u32[]{:S(2)}, u32[]{:S(2)}) collective-permute-start(f32[7,2,128,128]{3,2,0,1:T(8,128)S(1)} %get-tuple-element.9), channel_id=1, source_target_pairs={{8,0},{16,8},{24,16},{9,1},{17,9},{25,17},{10,2},{18,10},{26,18},{... | collective-permute-start | bytes 2752520 | tf_op jit(solution)/shard_map/ppermute | solution.py:24
  4.6 39.7 %collective-permute-start.1 = (f32[7,2,128,128]{3,2,0,1:T(8,128)S(1)}, f32[7,2,128,128]{3,2,0,1:T(8,128)S(1)}, u32[]{:S(2)}, u32[]{:S(2)}) collective-permute-start(f32[7,2,128,128]{3,2,0,1:T(8,128)S(1)} %get-tuple-element.10), channel_id=1, source_target_pairs={{0,8},{8,16},{16,24},{1,9},{9,17},{17,25},{2,10},{10,18},{18,26},{... | collective-permute-start | bytes 2752520 | tf_op jit(solution)/shard_map/ppermute | solution.py:22
  44.3 7.5 %copy-start.3 = (f32[8,1,2,128,128]{4,3,2,1,0:T(8,128)S(1)}, f32[8,1,2,128,128]{4,3,2,1,0:T(8,128)}, u32[]{:S(2)}) copy-start(f32[8,1,2,128,128]{4,3,2,1,0:T(8,128)} %param.7) | copy-start | bytes 3145732
  47.2 16.3 %collective-permute-start.2 = (f32[8,1,2,128,128]{4,3,0,2,1:T(8,128)S(1)}, f32[8,1,2,128,128]{4,3,0,2,1:T(8,128)S(1)}, u32[]{:S(2)}, u32[]{:S(2)}) collective-permute-start(f32[8,1,2,128,128]{4,3,0,2,1:T(8,128)S(1)} %bitcast.162), channel_id=1, source_target_pairs={{0,1},{1,2},{2,3},{3,4},{4,5},{5,6},{6,7},{8,9},{9,10},{10,11},{11... | collective-permute-start | bytes 3145736 | tf_op jit(solution)/shard_map/ppermute | solution.py:22
  51.9 11.6 %copy-start.1 = (f32[1,128,128]{2,1,0:T(8,128)S(1)}, f32[1,128,128]{2,1,0:T(8,128)}, u32[]{:S(2)}) copy-start(f32[1,128,128]{2,1,0:T(8,128)} %param.9) | copy-start | bytes 196612
  51.9 16.2 %collective-permute-start.3 = (f32[8,1,2,128,128]{4,3,0,2,1:T(8,128)S(1)}, f32[8,1,2,128,128]{4,3,0,2,1:T(8,128)S(1)}, u32[]{:S(2)}, u32[]{:S(2)}) collective-permute-start(f32[8,1,2,128,128]{4,3,0,2,1:T(8,128)S(1)} %bitcast.163), channel_id=1, source_target_pairs={{1,0},{2,1},{3,2},{4,3},{5,4},{6,5},{7,6},{9,8},{10,9},{11,10},{12... | collective-permute-start | bytes 3145736 | tf_op jit(solution)/shard_map/ppermute | solution.py:24
  64.6 3.6 %copy-start.2 = (f32[1,128,128]{2,1,0:T(8,128)S(1)}, f32[1,128,128]{2,1,0:T(8,128)}, u32[]{:S(2)}) copy-start(f32[1,128,128]{2,1,0:T(8,128)} %param.10) | copy-start | bytes 196612
  78.9 20.5 %collective-permute-start.4 = (f32[7,2,128,128]{3,2,0,1:T(8,128)S(1)}, f32[7,2,128,128]{3,2,0,1:T(8,128)S(1)}, u32[]{:S(2)}, u32[]{:S(2)}) collective-permute-start(f32[7,2,128,128]{3,2,0,1:T(8,128)S(1)} %get-tuple-element.7), channel_id=1, source_target_pairs={{8,0},{16,8},{24,16},{9,1},{17,9},{25,17},{10,2},{18,10},{26,18},{... | collective-permute-start | bytes 2752520 | tf_op jit(solution)/shard_map/ppermute | solution.py:24
  80.9 28.4 %collective-permute-start.5 = (f32[7,2,128,128]{3,2,0,1:T(8,128)S(1)}, f32[7,2,128,128]{3,2,0,1:T(8,128)S(1)}, u32[]{:S(2)}, u32[]{:S(2)}) collective-permute-start(f32[7,2,128,128]{3,2,0,1:T(8,128)S(1)} %get-tuple-element.8), channel_id=1, source_target_pairs={{0,8},{8,16},{16,24},{1,9},{9,17},{17,25},{2,10},{10,18},{18,26},{... | collective-permute-start | bytes 2752520 | tf_op jit(solution)/shard_map/ppermute | solution.py:22
  112.6 24.5 %collective-permute-start.6 = (f32[8,1,2,128,128]{4,3,0,2,1:T(8,128)S(1)}, f32[8,1,2,128,128]{4,3,0,2,1:T(8,128)S(1)}, u32[]{:S(2)}, u32[]{:S(2)}) collective-permute-start(f32[8,1,2,128,128]{4,3,0,2,1:T(8,128)S(1)} %bitcast.160), channel_id=1, source_target_pairs={{0,1},{1,2},{2,3},{3,4},{4,5},{5,6},{6,7},{8,9},{9,10},{10,11},{11... | collective-permute-start | bytes 3145736 | tf_op jit(solution)/shard_map/ppermute | solution.py:22
  125.4 16.1 %collective-permute-start.7 = (f32[8,1,2,128,128]{4,3,0,2,1:T(8,128)S(1)}, f32[8,1,2,128,128]{4,3,0,2,1:T(8,128)S(1)}, u32[]{:S(2)}, u32[]{:S(2)}) collective-permute-start(f32[8,1,2,128,128]{4,3,0,2,1:T(8,128)S(1)} %bitcast.161), channel_id=1, source_target_pairs={{1,0},{2,1},{3,2},{4,3},{5,4},{6,5},{7,6},{9,8},{10,9},{11,10},{12... | collective-permute-start | bytes 3145736 | tf_op jit(solution)/shard_map/ppermute | solution.py:24
where the time goes:
time: 155 us; the launch traced here: 153 us
  waiting for transfers between devices  81.8 us (53%)
  starting transfers between devices  32 us (21%)
  matrix products  29.2 us (19%)
  other arithmetic  6.48 us (4%)
  local copies, waits for them, and re-layouts  3.37 us (2%)
    ppermute x4, waiting for transfers between devices, with_halo(): lax.ppermute(tail, axis, [(i, (i + 1) % count) for i in range(ends)])  44.7 us
    ppermute x4, waiting for transfers between devices, with_halo(): lax.ppermute(head, axis, [((i + 1) % count, i) for i in range(ends)])  37.2 us
    ppermute x4, starting transfers between devices, with_halo(): lax.ppermute(tail, axis, [(i, (i + 1) % count) for i in range(ends)])  23 us
    ppermute x4, starting transfers between devices, with_halo(): lax.ppermute(head, axis, [((i + 1) % count, i) for i in range(ends)])  8.96 us
    dot_general x8, matrix products, matmul_adjoint(): return jnp.einsum('eij,ekj->eik', left, right, precision=HIGH)  8.65 us
    dot_general x8, matrix products, matmul_plain(): return jnp.einsum('eij,ejk->eik', left, right, precision=HIGH)  8.25 us
    dot_general x6, matrix products, sandwich(): half_done = jnp.einsum('ij,ecjk->ecik', coupling, values, precision=HIGH)  6.37 us
    dot_general x6, matrix products, sandwich(): return jnp.einsum('ecik,lk->ecil', half_done, coupling, precision=HIGH)  5.93 us
  transfers between devices with their start and end apart: 8, of which 8 were waited for; matrix products, arithmetic and copies ran while one was open for 6% of the time, Pallas kernels for 0%

commit v1 on v0

v1 whole, which is shorter than its diff:
```python
import functools

import jax
import jax.numpy as jnp
from jax import lax
from jax.experimental import pallas as pl
from jax.experimental.pallas import tpu as pltpu
from jax.sharding import PartitionSpec as P

SHIFT_NEAR = 3
SHIFT_FAR = 7
ITERS = 2

MESH = pl.DeviceIdType.MESH
F32 = jnp.float32
BF16 = jnp.bfloat16


def split(x):
    hi = x.astype(BF16)
    lo = (x - hi.astype(F32)).astype(BF16)
    return hi, lo


def dot(a, b, rhs_contract=0):
    return lax.dot_general(a, b, (((1,), (rhs_contract,)), ((), ())), preferred_element_type=F32)


def plan(count):
    half = count // 2
    pairs = [[half - 1 - p, half + p] for p in range(half)]
    if count % 2:
        pairs.append([count - 1])
    order = [e for pair in pairs for e in pair]
    first = list(range(half - 1, -1, -1))
    rest = list(range(half, count))
    to_left = [e for e in first + rest if e < SHIFT_FAR]
    mirror = [count - 1 - e for e in first + rest]
    to_right = [e for e in mirror if e >= count - SHIFT_FAR]
    return pairs, to_left, to_right


def kernel(
    counts, weights, green, retarded, c_on, c_low, c_up, out,
    halo, rim, mixed, middle, c_right, c_left, r_left, r_right,
    e_send, e_recv, s_send, s_recv,
):
    n_energy, n_slab = counts
    energies, _, size, _ = green.shape
    d = lax.axis_index("energy")
    s = lax.axis_index("slab")
    pairs, to_left, to_right = plan(energies)
    slot_right = {e: i for i, e in enumerate(to_left)}
    slot_left = {e: i for i, e in enumerate(to_right)}

    has = {("energy", 0): d > 0, ("energy", 1): d < n_energy - 1, ("slab", 0): s > 0, ("slab", 1): s < n_slab - 1}
    at = {"energy": d, "slab": s}
    sides = (0, 1)

    def peer(axis, side):
        return {axis: at[axis] + (1 if side else -1)}

    barrier = pltpu.get_barrier_semaphore()
    for axis in ("energy", "slab"):
        for side in sides:
            @pl.when(has[axis, side])
            def _(axis=axis, side=side):
                pl.semaphore_signal(barrier, inc=1, device_id=peer(axis, side), device_id_type=MESH)
    total = sum(jnp.where(flag, 1, 0) for flag in has.values())
    pl.semaphore_wait(barrier, total)

    def energy_copy(step, side, slot, block):
        return pltpu.make_async_remote_copy(
            src_ref=block, dst_ref=halo.at[step, 1 - side, slot],
            send_sem=e_send.at[step, side, slot], recv_sem=e_recv.at[step, 1 - side, slot],
            device_id=peer("energy", side), device_id_type=MESH,
        )

    def slab_copy(step, side, e):
        return pltpu.make_async_remote_copy(
            src_ref=mixed.at[step, e], dst_ref=rim.at[step, 1 - side, e],
            send_sem=s_send.at[step, side, e], recv_sem=s_recv.at[step, 1 - side, e],
            device_id=peer("slab", side), device_id_type=MESH,
        )

    def held(step):
        return green if step == 0 else middle.at[step - 1]

    def send_energy(step, side, slot):
        e = (to_left, to_right)[side][slot]
        energy_copy(step, side, slot, held(step).at[e]).start()

    @pl.when(has["energy", 0])
    def _():
        for slot in range(len(to_left)):
            send_energy(0, 0, slot)

    @pl.when(has["energy", 1])
    def _():
        for slot in range(len(to_right)):
            send_energy(0, 1, slot)

    for side in sides:
        @pl.when(jnp.logical_not(has["energy", side]))
        def _(side=side):
            halo[:, side] = jnp.zeros_like(halo[:, side])

        @pl.when(jnp.logical_not(has["slab", side]))
        def _(side=side):
            rim[:, side] = jnp.zeros_like(rim[:, side])

    highs, lows = [], []
    for j, ref in enumerate((c_low, c_on, c_up)):
        hi, lo = split(ref[0])
        c_right[j] = jnp.concatenate(
            [jnp.concatenate([hi, hi], 1), jnp.concatenate([lo, lo], 1)], 0)
        highs.append(hi)
        lows.append(lo)
    c_left[...] = jnp.concatenate([jnp.concatenate(highs, 1), jnp.concatenate(lows, 1)], 0)

    @pl.loop(0, energies)
    def _(e):
        re_hi, re_lo = split(retarded[e, 0])
        im_hi, im_lo = split(retarded[e, 1])
        top_hi = jnp.concatenate([re_hi, im_hi], 1)
        top_lo = jnp.concatenate([re_lo, im_lo], 1)
        r_left[e] = jnp.concatenate([top_hi, top_lo], 0)
        r_right[e, 0] = jnp.concatenate([top_hi, jnp.concatenate([-im_hi, re_hi], 1)], 0)
        r_right[e, 1] = jnp.concatenate([top_lo, jnp.concatenate([-im_lo, re_lo], 1)], 0)

    waited = {}

    def wait_halo(step, e):
        need = set()
        for shift in (-SHIFT_FAR, -SHIFT_NEAR, SHIFT_NEAR, SHIFT_FAR):
            at_e = e - shift
            if at_e < 0:
                need.add((0, slot_left[at_e + energies]))
            elif at_e >= energies:
                need.add((1, slot_right[at_e - energies]))
        for side, slot in sorted(need):
            for upto in range(waited.get((step, side), 0), slot + 1):
                @pl.when(has["energy", side])
                def _(side=side, upto=upto):
                    energy_copy(step, 1 - side, upto, held(step).at[0]).wait_recv()
            waited[step, side] = max(waited.get((step, side), 0), slot + 1)

    def part(step, e):
        if e < 0:
            return halo[step, 0, slot_left[e + energies]]
        if e >= energies:
            return halo[step, 1, slot_right[e - energies]]
        return held(step)[e]

    def mix(step, pair):
        for e in pair:
            wait_halo(step, e)
            total = weights[0] * part(step, e + SHIFT_FAR)
            total = total + weights[1] * part(step, e + SHIFT_NEAR)
            total = total + weights[2] * part(step, e - SHIFT_NEAR)
            total = total + weights[3] * part(step, e - SHIFT_FAR)
            mixed[step, e] = total
            for side in sides:
                @pl.when(has["slab", side])
                def _(side=side, e=e):
                    slab_copy(step, side, e).start()

    def two(lhs, rhs, contract):
        both = dot(lhs, rhs[0], contract)
        m = both.shape[0] // 2
        return both[:m] + both[m:] + dot(lhs[:m], rhs[1], contract)

    def solve(step, e):
        for side in sides:
            @pl.when(has["slab", side])
            def _(side=side):
                slab_copy(step, 1 - side, e).wait_recv()
        rights = []
        for j, block in enumerate((rim[step, 0, e], mixed[step, e], rim[step, 1, e])):
            hi, lo = split(block.reshape(2 * size, size))
            half = dot(jnp.concatenate([hi, lo], 1), c_right[j], 1)
            half = half[:, :size] + half[:, size:]
            rights.append(jnp.concatenate([half[:size], half[size:]], 1))
        sigma = two(c_left[...], split(jnp.concatenate(rights, 0)), 0)
        s_hi, s_lo = split(sigma)
        turned = [jnp.concatenate([v, jnp.concatenate([-v[:, size:], v[:, :size]], 1)], 0) for v in (s_hi, s_lo)]
        product = two(r_left[e], turned, 0)
        p_hi, p_lo = split(product)
        result = two(jnp.concatenate([p_hi, p_lo], 0), (r_right[e, 0], r_right[e, 1]), 1)
        target = out if step == ITERS - 1 else middle.at[step]
        target[e, 0] = result[:, :size]
        target[e, 1] = result[:, size:]

    sent = {}

    def pass_on(step, done):
        for side in sides:
            order = (to_left, to_right)[side]
            start = sent.get((step, side), 0)
            stop = start
            while stop < len(order) and order[stop] in done:
                stop += 1
            if stop > start:
                @pl.when(has["energy", side])
                def _(side=side, start=start, stop=stop):
                    for slot in range(start, stop):
                        send_energy(step, side, slot)
            sent[step, side] = stop

    last = len(pairs) - 1
    schedule = [("mix", 0), ("solve", 0)]
    for p in range(1, last + 1):
        schedule.append(("mix", p))
        if p >= 2:
            schedule.append(("solve", p - 1))
    schedule.append(("solve", last))
    if last == 0:
        schedule = [("mix", 0), ("solve", 0)]

    for step in range(ITERS):
        done = set()
        for what, p in schedule:
            if what == "mix":
                mix(step, pairs[p])
            else:
                for e in pairs[p]:
                    solve(step, e)
                done.update(pairs[p])
                if step < ITERS - 1:
                    pass_on(step + 1, done)

    for step in range(ITERS):
        for side in sides:
            @pl.when(has["energy", side])
            def _(side=side):
                for slot in range(len(to_left)):
                    energy_copy(step, side, slot, held(step).at[0]).wait_send()

            @pl.when(has["slab", side])
            def _(side=side):
                for e in range(energies):
                    slab_copy(step, side, e).wait_send()


def solution(mesh):
    counts = (mesh.shape["energy"], mesh.shape["slab"])

    def local(green_init, retarded, coupling_on, coupling_lower, coupling_upper, phonon_weights):
        current = green_init[:, 0]
        local_ret = retarded[:, 0]
        energies, _, size, _ = current.shape
        block = (2, size, size)
        vmem = pl.BlockSpec(memory_space=pltpu.VMEM)
        dma = pltpu.SemaphoreType.DMA
        result = pl.pallas_call(
            functools.partial(kernel, counts),
            out_shape=jax.ShapeDtypeStruct(current.shape, F32),
            in_specs=[pl.BlockSpec(memory_space=pltpu.SMEM)] + [vmem] * 5,
            out_specs=vmem,
            scratch_shapes=[
                pltpu.VMEM((ITERS, 2, SHIFT_FAR) + block, F32),
                pltpu.VMEM((ITERS, 2, energies) + block, F32),
                pltpu.VMEM((ITERS, energies) + block, F32),
                pltpu.VMEM((ITERS - 1, energies) + block, F32),
                pltpu.VMEM((3, 2 * size, 2 * size), BF16),
                pltpu.VMEM((2 * size, 3 * size), BF16),
                pltpu.VMEM((energies, 2 * size, 2 * size), BF16),
                pltpu.VMEM((energies, 2, 2 * size, 2 * size), BF16),
                dma((ITERS, 2, SHIFT_FAR)),
                dma((ITERS, 2, SHIFT_FAR)),
                dma((ITERS, 2, energies)),
                dma((ITERS, 2, energies)),
            ],
            compiler_params=pltpu.CompilerParams(
                collective_id=0, has_side_effects=True, vmem_limit_bytes=48 * 1024 * 1024),
        )(phonon_weights, current, local_ret, coupling_on, coupling_lower, coupling_upper)
        return result[:, None]

    in_specs = (
        P("energy", "slab", None, None, None),
        P("energy", "slab", None, None, None),
        P("slab", None, None),
        P("slab", None, None),
        P("slab", None, None),
        P(),
    )
    out_specs = P("energy", "slab", None, None, None)
    return jax.shard_map(local, mesh=mesh, in_specs=in_specs, out_specs=out_specs, check_vma=False)
```

time: 155 us -> 98.7 us (0.64)
  Pallas kernels: 0 us -> 91.8 us
  waiting for transfers between devices: 81.8 us -> 0 us
  starting transfers between devices: 32 us -> 0 us
  matrix products: 29.2 us -> 0 us
  other arithmetic: 6.48 us -> 0 us
  local copies, waits for them, and re-layouts: 3.37 us -> 6.59 us
    pallas_call x0 -> x1, Pallas kernels: none -> 91.8 us  [local(): pl.pallas_call(functools.partial(kernel, counts), out_shape=jax.ShapeDtyp...]
    ppermute x8 -> x0, waiting for transfers between devices: 81.8 us -> none  [the longest x4 44.7 us: with_halo(): lax.ppermute(tail, axis, [(i, (i + 1) % count) for i in range(ends)])]
    ppermute x8 -> x0, starting transfers between devices: 32 us -> none  [the longest x4 23 us: with_halo(): lax.ppermute(tail, axis, [(i, (i + 1) % count) for i in range(ends)])]
    dot_general x28 -> x0, matrix products: 29.2 us -> none  [the longest x8 8.65 us: matmul_adjoint(): return jnp.einsum('eij,ekj->eik', left, right, precision=HIGH)]
    add x2 -> x0, other arithmetic: 5.71 us -> none  [local(): mixture = mixture + phonon_weights[3] * lower_far]
    unnamed x12 -> x13, local copies, waits for them, and re-layouts: 1.44 us -> 6.59 us
  transfers between devices with their start and end apart: 8 -> 0, of which waited for: 8 -> 0; matrix products, arithmetic and copies ran while one was open for 6% -> 0% of each run, Pallas kernels for 0% -> 0%
where the time goes in v1:
time: 98.7 us; the launch traced here: 98.4 us
  Pallas kernels  91.8 us (93%)
  local copies, waits for them, and re-layouts  6.59 us (7%)
    pallas_call x1, Pallas kernels, local(): pl.pallas_call(functools.partial(kernel, counts), out_shape=jax.ShapeDtyp...  91.8 us
    unnamed x13, local copies, waits for them, and re-layouts  6.59 us

profile of v1, /device:TPU:5, one launch (start us, length us, event | category | flops | bytes accessed | tf_op | source)
XLA Modules:
  0.0 98.4 jit_solution(14297213131240110217)
XLA Ops:
  0.0 0.0 copy-start.5
  0.0 0.7 copy-done.5
  0.7 0.0 copy-start
  0.7 1.2 %copy-done = f32[8,1,2,128,128]{4,3,2,1,0:T(8,128)S(1)} copy-done((f32[8,1,2,128,128]{4,3,2,1,0:T(8,128)S(1)}, f32[8,1,2,128,128]{4,3,2,1,0:T(8,128)}, u32[]{:S(2)}) %copy-start) | copy-done | bytes 1048600
  1.9 0.0 copy-start.1
  1.9 1.2 %copy-done.1 = f32[8,1,2,128,128]{4,3,2,1,0:T(8,128)S(1)} copy-done((f32[8,1,2,128,128]{4,3,2,1,0:T(8,128)S(1)}, f32[8,1,2,128,128]{4,3,2,1,0:T(8,128)}, u32[]{:S(2)}) %copy-start.1) | copy-done | bytes 1048600
  3.1 0.0 copy-start.2
  3.1 0.8 copy-done.2
  3.9 0.0 copy-start.3
  3.9 0.8 copy-done.3
  4.8 0.0 copy-start.4
  4.8 0.8 copy-done.4
  5.6 91.8 %shard_map.64 = f32[8,2,128,128]{3,2,1,0:T(8,128)S(1)} custom-call(f32[4]{0:T(128)S(1)} %copy-done.5, f32[8,2,128,128]{3,2,1,0:T(8,128)S(1)} %bitcast.6, f32[8,2,128,128]{3,2,1,0:T(8,128)S(1)} %bitcast.7, f32[1,128,128]{2,1,0:T(8,128)S(1)} %copy-done.2, f32[1,128,128]{2,1,0:T(8,128)S(1)} %copy-done.3, f32[1,128,128]{2,1,0:T(8,128)S(1)} %copy-done.4), custom_call_target="tpu_custom_call" | custom-call | tf_op jit(solution)/shard_map/pallas_call | solution.py:255
  97.4 1.0 copy.9
Async XLA Ops:
  0.0 0.7 copy-start.5
  0.7 1.2 %copy-start = (f32[8,1,2,128,128]{4,3,2,1,0:T(8,128)S(1)}, f32[8,1,2,128,128]{4,3,2,1,0:T(8,128)}, u32[]{:S(2)}) copy-start(f32[8,1,2,128,128]{4,3,2,1,0:T(8,128)} %param.6) | copy-start | bytes 3145732
  1.9 1.2 %copy-start.1 = (f32[8,1,2,128,128]{4,3,2,1,0:T(8,128)S(1)}, f32[8,1,2,128,128]{4,3,2,1,0:T(8,128)}, u32[]{:S(2)}) copy-start(f32[8,1,2,128,128]{4,3,2,1,0:T(8,128)} %param.7) | copy-start | bytes 3145732
  3.1 0.8 copy-start.2
  3.9 0.8 copy-start.3
  4.8 0.8 copy-start.4

commit v2 on v1

v2 whole, which is shorter than its diff:
```python
import functools

import jax
import jax.numpy as jnp
from jax import lax
from jax.experimental import pallas as pl
from jax.experimental.pallas import tpu as pltpu
from jax.sharding import PartitionSpec as P

SHIFT_NEAR = 3
SHIFT_FAR = 7
ITERS = 2

MESH = pl.DeviceIdType.MESH
F32 = jnp.float32
BF16 = jnp.bfloat16


def split(x):
    hi = x.astype(BF16)
    lo = (x - hi.astype(F32)).astype(BF16)
    return hi, lo


def dot(a, b, rhs_contract=0):
    return lax.dot_general(a, b, (((1,), (rhs_contract,)), ((), ())), preferred_element_type=F32)


def needs(e, count):
    found = []
    for shift in (-SHIFT_FAR, -SHIFT_NEAR, SHIFT_NEAR, SHIFT_FAR):
        if e - shift < 0:
            found.append((0, e - shift + count))
        elif e - shift >= count:
            found.append((1, e - shift - count))
    return found


def by_arrival(count, arrivals):
    def ready(e):
        return max([arrivals[side].index(p) for side, p in needs(e, count) if side in arrivals], default=-1)

    order = sorted(range(count), key=lambda e: (ready(e), -e))
    return [order[i:i + 2] for i in range(0, count, 2)]


def inner_first(count):
    half = count // 2
    return list(range(half, count)) + list(range(half - 1, -1, -1))


class Role:
    def __init__(self, when, pairs, arrivals, sends, forwards=None, early=0):
        self.when, self.pairs, self.arrivals = when, pairs, arrivals
        self.sends, self.forwards, self.early = sends, forwards, early
        self.waited, self.sent = {}, {}


def kernel(
    counts, weights, green, retarded, c_on, c_low, c_up, out,
    halo, rim, mixed, middle, c_right, c_left, r_left, r_right,
    e_send, e_recv, s_send, s_recv,
):
    n_energy, n_slab = counts
    energies, _, size, _ = green.shape
    d = lax.axis_index("energy")
    s = lax.axis_index("slab")
    sides = (0, 1)
    has_slab = (s > 0, s < n_slab - 1)
    square = n_energy == 4
    upper = inner_first(energies)
    to_right = [e for e in upper if e >= energies - SHIFT_FAR]
    to_left = [energies - 1 - e for e in to_right]

    if square:
        flip = d >= 2
        is_end = jnp.logical_or(d == 0, d == n_energy - 1)
        is_mid = jnp.logical_not(is_end)
        x_peer = {"energy": d + 1 - 2 * (d % 2)}
        y_peer = {"energy": d + 2 - 4 * (d // 2)}
        peers = [(None, x_peer), (None, y_peer)]
        extra = [e for e in to_left if e not in to_right]
        mid_send = to_right[:2] + extra + to_right[2:]
        end_arrivals = {1: mid_send}
        end_pairs = by_arrival(energies, end_arrivals)
        end_send = [e for pair in end_pairs for e in pair if e >= energies - SHIFT_FAR]
        mid_arrivals = {0: end_send, 1: [energies - 1 - e for e in mid_send if e in to_right]}
        upper_pairs = [[energies - 1 - e, e] for e in upper[:energies // 2]]
        if energies % 2:
            upper_pairs = by_arrival(energies, mid_arrivals)
        roles = [
            Role(is_end, end_pairs, end_arrivals, [(None, x_peer, end_send, 0)], (1, y_peer, to_right), 4),
            Role(is_mid, upper_pairs, mid_arrivals, [(None, x_peer, mid_send, 1)]),
        ]
        empty = [(is_end, 0)]
        have = {}
    else:
        flip = None
        left, right = {"energy": d - 1}, {"energy": d + 1}
        has_left, has_right = d > 0, d < n_energy - 1
        peers = [(has_left, left), (has_right, right)]
        arrivals = {0: to_right, 1: to_left}
        roles = [Role(None, by_arrival(energies, arrivals), arrivals,
                      [(has_left, left, to_left, 1), (has_right, right, to_right, 0)])]
        empty = [(jnp.logical_not(has_left), 0), (jnp.logical_not(has_right), 1)]
        have = {0: has_left, 1: has_right}

    def when(flag, body):
        if flag is None:
            body()
        else:
            pl.when(flag)(body)

    def real(e):
        return e if flip is None else jnp.where(flip, energies - 1 - e, e)

    slabs = [(has_slab[0], {"slab": s - 1}), (has_slab[1], {"slab": s + 1})]
    barrier = pltpu.get_barrier_semaphore()
    total = 0
    for flag, to in peers + slabs:
        def greet(to=to):
            pl.semaphore_signal(barrier, inc=1, device_id=to, device_id_type=MESH)
        when(flag, greet)
        total = total + (1 if flag is None else jnp.where(flag, 1, 0))
    pl.semaphore_wait(barrier, total)

    def held(step, e):
        return green.at[real(e)] if step == 0 else middle.at[step - 1, e]

    def energy_copy(step, lane, src, to, side, slot):
        return pltpu.make_async_remote_copy(
            src_ref=src, dst_ref=halo.at[step, side, slot],
            send_sem=e_send.at[step, lane, slot], recv_sem=e_recv.at[step, side, slot],
            device_id=to, device_id_type=MESH,
        )

    def slab_copy(step, side, e):
        return pltpu.make_async_remote_copy(
            src_ref=mixed.at[step, e], dst_ref=rim.at[step, 1 - side, e],
            send_sem=s_send.at[step, side, e], recv_sem=s_recv.at[step, 1 - side, e],
            device_id=slabs[side][1], device_id_type=MESH,
        )

    def pass_on(role, step, done):
        for lane, (flag, to, order, side) in enumerate(role.sends):
            start = stop = role.sent.get((step, lane), 0)
            while stop < len(order) and order[stop] in done:
                stop += 1

            def send(lane=lane, to=to, todo=order[start:stop], side=side):
                for e in todo:
                    energy_copy(step, lane, held(step, e), to, side, e).start()
            if stop > start:
                when(flag, send)
            role.sent[step, lane] = stop

    def await_halo(role, step, side, upto):
        start = role.waited.get((step, side), 0)
        if upto <= start:
            return
        role.waited[step, side] = upto

        def wait():
            for slot in role.arrivals[side][start:upto]:
                block = halo.at[step, side, slot]
                energy_copy(step, 0, block, peers[0][1], side, slot).wait_recv()
                if role.forwards and role.forwards[0] == side and slot in role.forwards[2]:
                    energy_copy(step, 1, block, role.forwards[1], 1, energies - 1 - slot).start()
        when(have.get(side), wait)

    for role in roles:
        when(role.when, lambda role=role: pass_on(role, 0, range(energies)))

    for flag, side in empty:
        @pl.when(flag)
        def _(side=side):
            halo[:, side] = jnp.zeros_like(halo[:, side])

    for side in sides:
        @pl.when(jnp.logical_not(has_slab[side]))
        def _(side=side):
            rim[:, side] = jnp.zeros_like(rim[:, side])

    highs, lows = [], []
    for j, ref in enumerate((c_low, c_on, c_up)):
        hi, lo = split(ref[0])
        c_right[j] = jnp.concatenate(
            [jnp.concatenate([hi, hi], 1), jnp.concatenate([lo, lo], 1)], 0)
        highs.append(hi)
        lows.append(lo)
    c_left[...] = jnp.concatenate([jnp.concatenate(highs, 1), jnp.concatenate(lows, 1)], 0)

    @pl.loop(0, energies)
    def _(e):
        re_hi, re_lo = split(retarded[real(e), 0])
        im_hi, im_lo = split(retarded[real(e), 1])
        top_hi = jnp.concatenate([re_hi, im_hi], 1)
        top_lo = jnp.concatenate([re_lo, im_lo], 1)
        r_left[e] = jnp.concatenate([top_hi, top_lo], 0)
        r_right[e, 0] = jnp.concatenate([top_hi, jnp.concatenate([-im_hi, re_hi], 1)], 0)
        r_right[e, 1] = jnp.concatenate([top_lo, jnp.concatenate([-im_lo, re_lo], 1)], 0)

    shares = [weights[k] if flip is None else jnp.where(flip, weights[3 - k], weights[k]) for k in range(4)]

    def part(step, e):
        if e < 0:
            return halo[step, 0, e + energies]
        if e >= energies:
            return halo[step, 1, e - energies]
        return held(step, e)[...]

    def mix(role, step, pair):
        for e in pair:
            for side, slot in needs(e, energies):
                if side in role.arrivals:
                    await_halo(role, step, side, role.arrivals[side].index(slot) + 1)
            total = shares[0] * part(step, e + SHIFT_FAR)
            total = total + shares[1] * part(step, e + SHIFT_NEAR)
            total = total + shares[2] * part(step, e - SHIFT_NEAR)
            total = total + shares[3] * part(step, e - SHIFT_FAR)
            mixed[step, e] = total
            for side in sides:
                @pl.when(has_slab[side])
                def _(side=side, e=e):
                    slab_copy(step, side, e).start()

    def two(lhs, rhs, contract):
        both = dot(lhs, rhs[0], contract)
        m = both.shape[0] // 2
        return both[:m] + both[m:] + dot(lhs[:m], rhs[1], contract)

    def solve(step, e):
        for side in sides:
            @pl.when(has_slab[side])
            def _(side=side):
                slab_copy(step, 1 - side, e).wait_recv()
        rights = []
        for j, block in enumerate((rim[step, 0, e], mixed[step, e], rim[step, 1, e])):
            hi, lo = split(block.reshape(2 * size, size))
            half = dot(jnp.concatenate([hi, lo], 1), c_right[j], 1)
            half = half[:, :size] + half[:, size:]
            rights.append(jnp.concatenate([half[:size], half[size:]], 1))
        sigma = two(c_left[...], split(jnp.concatenate(rights, 0)), 0)
        s_hi, s_lo = split(sigma)
        turned = [jnp.concatenate([v, jnp.concatenate([-v[:, size:], v[:, :size]], 1)], 0) for v in (s_hi, s_lo)]
        product = two(r_left[e], turned, 0)
        p_hi, p_lo = split(product)
        result = two(jnp.concatenate([p_hi, p_lo], 0), (r_right[e, 0], r_right[e, 1]), 1)
        target = out.at[real(e)] if step == ITERS - 1 else middle.at[step, e]
        target[0] = result[:, :size]
        target[1] = result[:, size:]

    last = len(roles[0].pairs) - 1
    schedule = [("mix", 0), ("solve", 0)]
    for p in range(1, last + 1):
        schedule.append(("mix", p))
        if p >= 2:
            schedule.append(("solve", p - 1))
    if last:
        schedule.append(("solve", last))

    for step in range(ITERS):
        for what, p in schedule:
            if what == "mix":
                for role in roles:
                    def do_mix(role=role):
                        mix(role, step, role.pairs[p])
                        if p == 0 and role.early:
                            side = role.forwards[0]
                            await_halo(role, step, side, min(role.early, len(role.arrivals[side])))
                    when(role.when, do_mix)
                continue
            for i in range(len(roles[0].pairs[p])):
                e = roles[-1].pairs[p][i]
                if len(roles) > 1:
                    e = jnp.where(roles[0].when, roles[0].pairs[p][i], e)
                solve(step, e)
            if step < ITERS - 1:
                for role in roles:
                    done = [e for pair in role.pairs[:p + 1] for e in pair]
                    when(role.when, lambda role=role, done=done: pass_on(role, step + 1, done))
        for role in roles:
            def rest(role=role):
                for side, order in role.arrivals.items():
                    await_halo(role, step, side, len(order))
            when(role.when, rest)

    for step in range(ITERS):
        for role in roles:
            def finish(role=role):
                for lane, (flag, to, order, side) in enumerate(role.sends):
                    def wait(lane=lane, to=to, order=order, side=side):
                        for e in order:
                            energy_copy(step, lane, held(step, e), to, side, e).wait_send()
                    when(flag, wait)
                if role.forwards:
                    for slot in role.forwards[2]:
                        energy_copy(
                            step, 1, halo.at[step, 1, slot], role.forwards[1], 1, energies - 1 - slot).wait_send()
            when(role.when, finish)
        for side in sides:
            @pl.when(has_slab[side])
            def _(side=side):
                for e in range(energies):
                    slab_copy(step, side, e).wait_send()


def solution(mesh):
    counts = (mesh.shape["energy"], mesh.shape["slab"])

    def local(green_init, retarded, coupling_on, coupling_lower, coupling_upper, phonon_weights):
        current = green_init[:, 0]
        local_ret = retarded[:, 0]
        energies, _, size, _ = current.shape
        block = (2, size, size)
        vmem = pl.BlockSpec(memory_space=pltpu.VMEM)
        dma = pltpu.SemaphoreType.DMA
        result = pl.pallas_call(
            functools.partial(kernel, counts),
            out_shape=jax.ShapeDtypeStruct(current.shape, F32),
            in_specs=[pl.BlockSpec(memory_space=pltpu.SMEM)] + [vmem] * 5,
            out_specs=vmem,
            scratch_shapes=[
                pltpu.VMEM((ITERS, 2, energies) + block, F32),
                pltpu.VMEM((ITERS, 2, energies) + block, F32),
                pltpu.VMEM((ITERS, energies) + block, F32),
                pltpu.VMEM((ITERS - 1, energies) + block, F32),
                pltpu.VMEM((3, 2 * size, 2 * size), BF16),
                pltpu.VMEM((2 * size, 3 * size), BF16),
                pltpu.VMEM((energies, 2 * size, 2 * size), BF16),
                pltpu.VMEM((energies, 2, 2 * size, 2 * size), BF16),
                dma((ITERS, 2, energies)),
                dma((ITERS, 2, energies)),
                dma((ITERS, 2, energies)),
                dma((ITERS, 2, energies)),
            ],
            compiler_params=pltpu.CompilerParams(
                collective_id=0, has_side_effects=True, vmem_limit_bytes=48 * 1024 * 1024),
        )(phonon_weights, current, local_ret, coupling_on, coupling_lower, coupling_upper)
        return result[:, None]

    in_specs = (
        P("energy", "slab", None, None, None),
        P("energy", "slab", None, None, None),
        P("slab", None, None),
        P("slab", None, None),
        P("slab", None, None),
        P(),
    )
    out_specs = P("energy", "slab", None, None, None)
    return jax.shard_map(local, mesh=mesh, in_specs=in_specs, out_specs=out_specs, check_vma=False)
```

time: 98.7 us -> 76.4 us (0.77)
  Pallas kernels: 91.8 us -> 69.4 us
    pallas_call x1, Pallas kernels: 91.8 us -> 69.4 us  [local(): pl.pallas_call(functools.partial(kernel, counts), out_shape=jax.ShapeDtyp...]
where the time goes in v2:
time: 76.4 us; the launch traced here: 76 us
  Pallas kernels  69.4 us (91%)
  local copies, waits for them, and re-layouts  6.59 us (9%)
    pallas_call x1, Pallas kernels, local(): pl.pallas_call(functools.partial(kernel, counts), out_shape=jax.ShapeDtyp...  69.4 us
    unnamed x13, local copies, waits for them, and re-layouts  6.59 us

profile of v2, /device:TPU:5, one launch (start us, length us, event | category | flops | bytes accessed | tf_op | source)
XLA Modules:
  0.0 76.0 jit_solution(2433073146314515191)
XLA Ops:
  0.0 0.0 copy-start.5
  0.0 0.7 copy-done.5
  0.7 0.0 copy-start
  0.7 1.2 %copy-done = f32[8,1,2,128,128]{4,3,2,1,0:T(8,128)S(1)} copy-done((f32[8,1,2,128,128]{4,3,2,1,0:T(8,128)S(1)}, f32[8,1,2,128,128]{4,3,2,1,0:T(8,128)}, u32[]{:S(2)}) %copy-start) | copy-done | bytes 1048600
  1.9 0.0 copy-start.1
  1.9 1.2 %copy-done.1 = f32[8,1,2,128,128]{4,3,2,1,0:T(8,128)S(1)} copy-done((f32[8,1,2,128,128]{4,3,2,1,0:T(8,128)S(1)}, f32[8,1,2,128,128]{4,3,2,1,0:T(8,128)}, u32[]{:S(2)}) %copy-start.1) | copy-done | bytes 1048600
  3.1 0.0 copy-start.2
  3.1 0.8 %copy-done.2 = f32[1,128,128]{2,1,0:T(8,128)S(1)} copy-done((f32[1,128,128]{2,1,0:T(8,128)S(1)}, f32[1,128,128]{2,1,0:T(8,128)}, u32[]{:S(2)}) %copy-start.2) | copy-done | bytes 65560
  3.9 0.0 copy-start.3
  3.9 0.8 %copy-done.3 = f32[1,128,128]{2,1,0:T(8,128)S(1)} copy-done((f32[1,128,128]{2,1,0:T(8,128)S(1)}, f32[1,128,128]{2,1,0:T(8,128)}, u32[]{:S(2)}) %copy-start.3) | copy-done | bytes 65560
  4.8 0.0 copy-start.4
  4.8 0.8 %copy-done.4 = f32[1,128,128]{2,1,0:T(8,128)S(1)} copy-done((f32[1,128,128]{2,1,0:T(8,128)S(1)}, f32[1,128,128]{2,1,0:T(8,128)}, u32[]{:S(2)}) %copy-start.4) | copy-done | bytes 65560
  5.6 69.4 %shard_map.64 = f32[8,2,128,128]{3,2,1,0:T(8,128)S(1)} custom-call(f32[4]{0:T(128)S(1)} %copy-done.5, f32[8,2,128,128]{3,2,1,0:T(8,128)S(1)} %bitcast.6, f32[8,2,128,128]{3,2,1,0:T(8,128)S(1)} %bitcast.7, f32[1,128,128]{2,1,0:T(8,128)S(1)} %copy-done.2, f32[1,128,128]{2,1,0:T(8,128)S(1)} %copy-done.3, f32[1,128,128]{2,1,0:T(8,128)S(1)} %copy-done.4), custom_call_target="tpu_custom_call" | custom-call | tf_op jit(solution)/shard_map/pallas_call | solution.py:318
  75.0 1.0 %copy.9 = f32[8,1,2,128,128]{4,3,2,1,0:T(8,128)} copy(f32[8,1,2,128,128]{4,3,2,1,0:T(8,128)S(1)} %bitcast.5) | data formatting | bytes 2097152
Async XLA Ops:
  0.0 0.7 copy-start.5
  0.7 1.2 %copy-start = (f32[8,1,2,128,128]{4,3,2,1,0:T(8,128)S(1)}, f32[8,1,2,128,128]{4,3,2,1,0:T(8,128)}, u32[]{:S(2)}) copy-start(f32[8,1,2,128,128]{4,3,2,1,0:T(8,128)} %param.6) | copy-start | bytes 3145732
  1.9 1.2 %copy-start.1 = (f32[8,1,2,128,128]{4,3,2,1,0:T(8,128)S(1)}, f32[8,1,2,128,128]{4,3,2,1,0:T(8,128)}, u32[]{:S(2)}) copy-start(f32[8,1,2,128,128]{4,3,2,1,0:T(8,128)} %param.7) | copy-start | bytes 3145732
  3.1 0.8 %copy-start.2 = (f32[1,128,128]{2,1,0:T(8,128)S(1)}, f32[1,128,128]{2,1,0:T(8,128)}, u32[]{:S(2)}) copy-start(f32[1,128,128]{2,1,0:T(8,128)} %c_on.1) | copy-start | bytes 196612
  3.9 0.8 %copy-start.3 = (f32[1,128,128]{2,1,0:T(8,128)S(1)}, f32[1,128,128]{2,1,0:T(8,128)}, u32[]{:S(2)}) copy-start(f32[1,128,128]{2,1,0:T(8,128)} %c_low.1) | copy-start | bytes 196612
  4.8 0.8 %copy-start.4 = (f32[1,128,128]{2,1,0:T(8,128)S(1)}, f32[1,128,128]{2,1,0:T(8,128)}, u32[]{:S(2)}) copy-start(f32[1,128,128]{2,1,0:T(8,128)} %c_up.1) | copy-start | bytes 196612

commit v3 on v2

--- a/solution.py
+++ b/solution.py
@@ -10,6 +10,9 @@
 SHIFT_NEAR = 3
 SHIFT_FAR = 7
 ITERS = 2
+
+LAG = 2
+POLLS = 2
 
 MESH = pl.DeviceIdType.MESH
 F32 = jnp.float32
@@ -36,12 +39,13 @@
     return found
 
 
-def by_arrival(count, arrivals):
+def by_arrival(count, arrivals, lead=0):
     def ready(e):
-        return max([arrivals[side].index(p) for side, p in needs(e, count) if side in arrivals], default=-1)
-
-    order = sorted(range(count), key=lambda e: (ready(e), -e))
-    return [order[i:i + 2] for i in range(0, count, 2)]
+        return max(
+            [arrivals[side].index(p) - (0 if side else lead) for side, p in needs(e, count) if side in arrivals],
+            default=-count)
+
+    return sorted(range(count), key=lambda e: (ready(e), -e))
 
 
 def inner_first(count):
@@ -50,9 +54,9 @@
 
 
 class Role:
-    def __init__(self, when, pairs, arrivals, sends, forwards=None, early=0):
-        self.when, self.pairs, self.arrivals = when, pairs, arrivals
-        self.sends, self.forwards, self.early = sends, forwards, early
+    def __init__(self, when, order, arrivals, sends, forwards=None):
+        self.when, self.order, self.arrivals = when, order, arrivals
+        self.sends, self.forwards = sends, forwards
         self.waited, self.sent = {}, {}
 
 
@@ -79,18 +83,21 @@
         x_peer = {"energy": d + 1 - 2 * (d % 2)}
         y_peer = {"energy": d + 2 - 4 * (d // 2)}
         peers = [(None, x_peer), (None, y_peer)]
+        half = energies // 2
         extra = [e for e in to_left if e not in to_right]
-        mid_send = to_right[:2] + extra + to_right[2:]
-        end_arrivals = {1: mid_send}
-        end_pairs = by_arrival(energies, end_arrivals)
-        end_send = [e for pair in end_pairs for e in pair if e >= energies - SHIFT_FAR]
-        mid_arrivals = {0: end_send, 1: [energies - 1 - e for e in mid_send if e in to_right]}
-        upper_pairs = [[energies - 1 - e, e] for e in upper[:energies // 2]]
-        if energies % 2:
-            upper_pairs = by_arrival(energies, mid_arrivals)
+        start = to_right[:2] + to_right[-1:] + to_right[2:-1]
+        later = [to_right[0]] + to_right[half - 1:half + 1] + to_right[1:half - 1] + to_right[half + 1:]
+        mid_send = [start + extra] + [later + extra] * (ITERS - 1)
+        end_arrivals = [{1: order} for order in mid_send]
+        end_order = [by_arrival(energies, arrivals) for arrivals in end_arrivals]
+        end_send = [start] + [[e for e in order if e in to_right] for order in end_order[:-1]]
+        mid_arrivals = [
+            {0: own, 1: [energies - 1 - e for e in order if e in to_right]}
+            for own, order in zip(end_send, mid_send)]
+        mid_order = [by_arrival(energies, arrivals, 2.5 if step else 1.5) for step, arrivals in enumerate(mid_arrivals)]
         roles = [
-            Role(is_end, end_pairs, end_arrivals, [(None, x_peer, end_send, 0)], (1, y_peer, to_right), 4),
-            Role(is_mid, upper_pairs, mid_arrivals, [(None, x_peer, mid_send, 1)]),
+            Role(is_end, end_order, end_arrivals, [(None, x_peer, end_send, 0)], (1, y_peer, to_right)),
+            Role(is_mid, mid_order, mid_arrivals, [(None, x_peer, mid_send, 1)]),
         ]
         empty = [(is_end, 0)]
         have = {}
@@ -100,8 +107,10 @@
         has_left, has_right = d > 0, d < n_energy - 1
         peers = [(has_left, left), (has_right, right)]
         arrivals = {0: to_right, 1: to_left}
-        roles = [Role(None, by_arrival(energies, arrivals), arrivals,
-                      [(has_left, left, to_left, 1), (has_right, right, to_right, 0)])]
+        every = range(ITERS)
+        roles = [Role(
+            None, [by_arrival(energies, arrivals) for _ in every], [arrivals for _ in every],
+            [(has_left, left, [to_left for _ in every], 1), (has_right, right, [to_right for _ in every], 0)])]
         empty = [(jnp.logical_not(has_left), 0), (jnp.logical_not(has_right), 1)]
         have = {0: has_left, 1: has_right}
 
@@ -142,7 +151,8 @@
         )
 
     def pass_on(role, step, done):
-        for lane, (flag, to, order, side) in enumerate(role.sends):
+        for lane, (flag, to, orders, side) in enumerate(role.sends):
+            order = orders[step]
             start = stop = role.sent.get((step, lane), 0)
             while stop < len(order) and order[stop] in done:
                 stop += 1
@@ -161,7 +171,7 @@
         role.waited[step, side] = upto
 
         def wait():
-            for slot in role.arrivals[side][start:upto]:
+            for slot in role.arrivals[step][side][start:upto]:
                 block = halo.at[step, side, slot]
                 energy_copy(step, 0, block, peers[0][1], side, slot).wait_recv()
                 if role.forwards and role.forwards[0] == side and slot in role.forwards[2]:
@@ -209,20 +219,19 @@
             return halo[step, 1, e - energies]
         return held(step, e)[...]
 
-    def mix(role, step, pair):
-        for e in pair:
-            for side, slot in needs(e, energies):
-                if side in role.arrivals:
-                    await_halo(role, step, side, role.arrivals[side].index(slot) + 1)
-            total = shares[0] * part(step, e + SHIFT_FAR)
-            total = total + shares[1] * part(step, e + SHIFT_NEAR)
-            total = total + shares[2] * part(step, e - SHIFT_NEAR)
-            total = total + shares[3] * part(step, e - SHIFT_FAR)
-            mixed[step, e] = total
-            for side in sides:
-                @pl.when(has_slab[side])
-                def _(side=side, e=e):
-                    slab_copy(step, side, e).start()
+    def mix(role, step, e):
+        for side, slot in needs(e, energies):
+            if side in role.arrivals[step]:
+                await_halo(role, step, side, role.arrivals[step][side].index(slot) + 1)
+        total = shares[0] * part(step, e + SHIFT_FAR)
+        total = total + shares[1] * part(step, e + SHIFT_NEAR)
+        total = total + shares[2] * part(step, e - SHIFT_NEAR)
+        total = total + shares[3] * part(step, e - SHIFT_FAR)
+        mixed[step, e] = total
+        for side in sides:
+            @pl.when(has_slab[side])
+            def _(side=side):
+                slab_copy(step, side, e).start()
 
     def two(lhs, rhs, contract):
         both = dot(lhs, rhs[0], contract)
@@ -250,46 +259,39 @@
         target[0] = result[:, :size]
         target[1] = result[:, size:]
 
-    last = len(roles[0].pairs) - 1
-    schedule = [("mix", 0), ("solve", 0)]
-    for p in range(1, last + 1):
-        schedule.append(("mix", p))
-        if p >= 2:
-            schedule.append(("solve", p - 1))
-    if last:
-        schedule.append(("solve", last))
-
     for step in range(ITERS):
-        for what, p in schedule:
-            if what == "mix":
+        for i in range(energies + LAG):
+            if i < energies:
                 for role in roles:
-                    def do_mix(role=role):
-                        mix(role, step, role.pairs[p])
-                        if p == 0 and role.early:
-                            side = role.forwards[0]
-                            await_halo(role, step, side, min(role.early, len(role.arrivals[side])))
-                    when(role.when, do_mix)
+                    when(role.when, lambda role=role: mix(role, step, role.order[step][i]))
+            at = i - LAG
+            if at < 0:
                 continue
-            for i in range(len(roles[0].pairs[p])):
-                e = roles[-1].pairs[p][i]
-                if len(roles) > 1:
-                    e = jnp.where(roles[0].when, roles[0].pairs[p][i], e)
-                solve(step, e)
+            ahead = at - energies + POLLS + 1
+            if step < ITERS - 1 and ahead > 0:
+                for role in roles:
+                    if role.forwards:
+                        side = role.forwards[0]
+                        when(role.when, lambda: await_halo(
+                            role, step + 1, side, min(ahead, len(role.arrivals[step + 1][side]))))
+            e = roles[-1].order[step][at]
+            if len(roles) > 1:
+                e = jnp.where(roles[0].when, roles[0].order[step][at], e)
+            solve(step, e)
             if step < ITERS - 1:
                 for role in roles:
-                    done = [e for pair in role.pairs[:p + 1] for e in pair]
-                    when(role.when, lambda role=role, done=done: pass_on(role, step + 1, done))
+                    when(role.when, lambda role=role: pass_on(role, step + 1, role.order[step][:at + 1]))
         for role in roles:
             def rest(role=role):
-                for side, order in role.arrivals.items():
+                for side, order in role.arrivals[step].items():
                     await_halo(role, step, side, len(order))
             when(role.when, rest)
 
     for step in range(ITERS):
         for role in roles:
             def finish(role=role):
-                for lane, (flag, to, order, side) in enumerate(role.sends):
-                    def wait(lane=lane, to=to, order=order, side=side):
+                for lane, (flag, to, orders, side) in enumerate(role.sends):
+                    def wait(lane=lane, to=to, order=orders[step], side=side):
                         for e in order:
                             energy_copy(step, lane, held(step, e), to, side, e).wait_send()
                     when(flag, wait)

time: 76.4 us -> 66 us (0.86)
  Pallas kernels: 69.4 us -> 58.9 us
    pallas_call x1, Pallas kernels: 69.4 us -> 58.9 us  [local(): pl.pallas_call(functools.partial(kernel, counts), out_shape=jax.ShapeDtyp...]
where the time goes in v3:
time: 66 us; the launch traced here: 65.5 us
  Pallas kernels  58.9 us (89%)
  local copies, waits for them, and re-layouts  6.59 us (10%)
    pallas_call x1, Pallas kernels, local(): pl.pallas_call(functools.partial(kernel, counts), out_shape=jax.ShapeDtyp...  58.9 us
    unnamed x13, local copies, waits for them, and re-layouts  6.59 us

profile of v3, /device:TPU:5, one launch (start us, length us, event | category | flops | bytes accessed | tf_op | source)
XLA Modules:
  0.0 65.5 jit_solution(9790862665545240693)
XLA Ops:
  0.0 0.0 copy-start.5
  0.0 0.7 copy-done.5
  0.7 0.0 copy-start
  0.7 1.2 %copy-done = f32[8,1,2,128,128]{4,3,2,1,0:T(8,128)S(1)} copy-done((f32[8,1,2,128,128]{4,3,2,1,0:T(8,128)S(1)}, f32[8,1,2,128,128]{4,3,2,1,0:T(8,128)}, u32[]{:S(2)}) %copy-start) | copy-done | bytes 1048600
  1.9 0.0 copy-start.1
  1.9 1.2 %copy-done.1 = f32[8,1,2,128,128]{4,3,2,1,0:T(8,128)S(1)} copy-done((f32[8,1,2,128,128]{4,3,2,1,0:T(8,128)S(1)}, f32[8,1,2,128,128]{4,3,2,1,0:T(8,128)}, u32[]{:S(2)}) %copy-start.1) | copy-done | bytes 1048600
  3.1 0.0 copy-start.2
  3.1 0.8 %copy-done.2 = f32[1,128,128]{2,1,0:T(8,128)S(1)} copy-done((f32[1,128,128]{2,1,0:T(8,128)S(1)}, f32[1,128,128]{2,1,0:T(8,128)}, u32[]{:S(2)}) %copy-start.2) | copy-done | bytes 65560
  3.9 0.0 copy-start.3
  3.9 0.8 %copy-done.3 = f32[1,128,128]{2,1,0:T(8,128)S(1)} copy-done((f32[1,128,128]{2,1,0:T(8,128)S(1)}, f32[1,128,128]{2,1,0:T(8,128)}, u32[]{:S(2)}) %copy-start.3) | copy-done | bytes 65560
  4.8 0.0 copy-start.4
  4.8 0.8 %copy-done.4 = f32[1,128,128]{2,1,0:T(8,128)S(1)} copy-done((f32[1,128,128]{2,1,0:T(8,128)S(1)}, f32[1,128,128]{2,1,0:T(8,128)}, u32[]{:S(2)}) %copy-start.4) | copy-done | bytes 65560
  5.6 58.9 %shard_map.64 = f32[8,2,128,128]{3,2,1,0:T(8,128)S(1)} custom-call(f32[4]{0:T(128)S(1)} %copy-done.5, f32[8,2,128,128]{3,2,1,0:T(8,128)S(1)} %bitcast.6, f32[8,2,128,128]{3,2,1,0:T(8,128)S(1)} %bitcast.7, f32[1,128,128]{2,1,0:T(8,128)S(1)} %copy-done.2, f32[1,128,128]{2,1,0:T(8,128)S(1)} %copy-done.3, f32[1,128,128]{2,1,0:T(8,128)S(1)} %copy-done.4), custom_call_target="tpu_custom_call" | custom-call | tf_op jit(solution)/shard_map/pallas_call | solution.py:320
  64.5 1.0 %copy.9 = f32[8,1,2,128,128]{4,3,2,1,0:T(8,128)} copy(f32[8,1,2,128,128]{4,3,2,1,0:T(8,128)S(1)} %bitcast.5) | data formatting | bytes 2097152
Async XLA Ops:
  0.0 0.7 %copy-start.5 = (f32[4]{0:T(128)S(1)}, f32[4]{0:T(128)}, u32[]{:S(2)}) copy-start(f32[4]{0:T(128)} %weights.1) | copy-start | bytes 52
  0.7 1.2 %copy-start = (f32[8,1,2,128,128]{4,3,2,1,0:T(8,128)S(1)}, f32[8,1,2,128,128]{4,3,2,1,0:T(8,128)}, u32[]{:S(2)}) copy-start(f32[8,1,2,128,128]{4,3,2,1,0:T(8,128)} %param.6) | copy-start | bytes 3145732
  1.9 1.2 %copy-start.1 = (f32[8,1,2,128,128]{4,3,2,1,0:T(8,128)S(1)}, f32[8,1,2,128,128]{4,3,2,1,0:T(8,128)}, u32[]{:S(2)}) copy-start(f32[8,1,2,128,128]{4,3,2,1,0:T(8,128)} %param.7) | copy-start | bytes 3145732
  3.1 0.8 %copy-start.2 = (f32[1,128,128]{2,1,0:T(8,128)S(1)}, f32[1,128,128]{2,1,0:T(8,128)}, u32[]{:S(2)}) copy-start(f32[1,128,128]{2,1,0:T(8,128)} %c_on.1) | copy-start | bytes 196612
  3.9 0.8 %copy-start.3 = (f32[1,128,128]{2,1,0:T(8,128)S(1)}, f32[1,128,128]{2,1,0:T(8,128)}, u32[]{:S(2)}) copy-start(f32[1,128,128]{2,1,0:T(8,128)} %c_low.1) | copy-start | bytes 196612
  4.8 0.8 %copy-start.4 = (f32[1,128,128]{2,1,0:T(8,128)S(1)}, f32[1,128,128]{2,1,0:T(8,128)}, u32[]{:S(2)}) copy-start(f32[1,128,128]{2,1,0:T(8,128)} %c_up.1) | copy-start | bytes 196612

commit v4 on v3

--- a/solution.py
+++ b/solution.py
@@ -61,7 +61,8 @@
 
 
 def kernel(
-    counts, weights, green, retarded, c_on, c_low, c_up, out,
+    counts, weights_in, green_in, retarded_in, on_in, low_in, up_in, out_hbm,
+    weights, green, retarded, c_on, c_low, c_up, out, load_sem, store_sem,
     halo, rim, mixed, middle, c_right, c_left, r_left, r_right,
     e_send, e_recv, s_send, s_recv,
 ):
@@ -123,6 +124,12 @@
     def real(e):
         return e if flip is None else jnp.where(flip, energies - 1 - e, e)
 
+    loads = [
+        pltpu.make_async_copy(src, dst, load_sem.at[i])
+        for i, (src, dst) in enumerate((
+            (low_in, c_low), (on_in, c_on), (up_in, c_up), (retarded_in, retarded),
+            (weights_in, weights), (green_in, green)))]
+
     slabs = [(has_slab[0], {"slab": s - 1}), (has_slab[1], {"slab": s + 1})]
     barrier = pltpu.get_barrier_semaphore()
     total = 0
@@ -136,6 +143,9 @@
     def held(step, e):
         return green.at[real(e)] if step == 0 else middle.at[step - 1, e]
 
+    def source(step, e):
+        return green_in.at[real(e)] if step == 0 else middle.at[step - 1, e]
+
     def energy_copy(step, lane, src, to, side, slot):
         return pltpu.make_async_remote_copy(
             src_ref=src, dst_ref=halo.at[step, side, slot],
@@ -159,7 +169,7 @@
 
             def send(lane=lane, to=to, todo=order[start:stop], side=side):
                 for e in todo:
-                    energy_copy(step, lane, held(step, e), to, side, e).start()
+                    energy_copy(step, lane, source(step, e), to, side, e).start()
             if stop > start:
                 when(flag, send)
             role.sent[step, lane] = stop
@@ -181,6 +191,9 @@
     for role in roles:
         when(role.when, lambda role=role: pass_on(role, 0, range(energies)))
 
+    for load in loads:
+        load.start()
+
     for flag, side in empty:
         @pl.when(flag)
         def _(side=side):
@@ -191,6 +204,8 @@
         def _(side=side):
             rim[:, side] = jnp.zeros_like(rim[:, side])
 
+    for load in loads[:3]:
+        load.wait()
     highs, lows = [], []
     for j, ref in enumerate((c_low, c_on, c_up)):
         hi, lo = split(ref[0])
@@ -199,6 +214,8 @@
         highs.append(hi)
         lows.append(lo)
     c_left[...] = jnp.concatenate([jnp.concatenate(highs, 1), jnp.concatenate(lows, 1)], 0)
+
+    loads[3].wait()
 
     @pl.loop(0, energies)
     def _(e):
@@ -210,6 +227,8 @@
         r_right[e, 0] = jnp.concatenate([top_hi, jnp.concatenate([-im_hi, re_hi], 1)], 0)
         r_right[e, 1] = jnp.concatenate([top_lo, jnp.concatenate([-im_lo, re_lo], 1)], 0)
 
+    for load in loads[4:]:
+        load.wait()
     shares = [weights[k] if flip is None else jnp.where(flip, weights[3 - k], weights[k]) for k in range(4)]
 
     def part(step, e):
@@ -232,6 +251,9 @@
             @pl.when(has_slab[side])
             def _(side=side):
                 slab_copy(step, side, e).start()
+
+    def store(e):
+        return pltpu.make_async_copy(out.at[e], out_hbm.at[real(e)], store_sem.at[e])
 
     def two(lhs, rhs, contract):
         both = dot(lhs, rhs[0], contract)
@@ -255,9 +277,11 @@
         product = two(r_left[e], turned, 0)
         p_hi, p_lo = split(product)
         result = two(jnp.concatenate([p_hi, p_lo], 0), (r_right[e, 0], r_right[e, 1]), 1)
-        target = out.at[real(e)] if step == ITERS - 1 else middle.at[step, e]
+        target = out.at[e] if step == ITERS - 1 else middle.at[step, e]
         target[0] = result[:, :size]
         target[1] = result[:, size:]
+        if step == ITERS - 1:
+            store(e).start()
 
     for step in range(ITERS):
         for i in range(energies + LAG):
@@ -287,13 +311,15 @@
                     await_halo(role, step, side, len(order))
             when(role.when, rest)
 
+    for e in range(energies):
+        store(e).wait()
     for step in range(ITERS):
         for role in roles:
             def finish(role=role):
                 for lane, (flag, to, orders, side) in enumerate(role.sends):
                     def wait(lane=lane, to=to, order=orders[step], side=side):
                         for e in order:
-                            energy_copy(step, lane, held(step, e), to, side, e).wait_send()
+                            energy_copy(step, lane, source(step, e), to, side, e).wait_send()
                     when(flag, wait)
                 if role.forwards:
                     for slot in role.forwards[2]:
@@ -315,14 +341,23 @@
         local_ret = retarded[:, 0]
         energies, _, size, _ = current.shape
         block = (2, size, size)
-        vmem = pl.BlockSpec(memory_space=pltpu.VMEM)
+        hbm = pl.BlockSpec(memory_space=pltpu.HBM)
         dma = pltpu.SemaphoreType.DMA
         result = pl.pallas_call(
             functools.partial(kernel, counts),
             out_shape=jax.ShapeDtypeStruct(current.shape, F32),
-            in_specs=[pl.BlockSpec(memory_space=pltpu.SMEM)] + [vmem] * 5,
-            out_specs=vmem,
+            in_specs=[hbm] * 6,
+            out_specs=hbm,
             scratch_shapes=[
+                pltpu.SMEM(phonon_weights.shape, F32),
+                pltpu.VMEM(current.shape, F32),
+                pltpu.VMEM(current.shape, F32),
+                pltpu.VMEM(coupling_on.shape, F32),
+                pltpu.VMEM(coupling_on.shape, F32),
+                pltpu.VMEM(coupling_on.shape, F32),
+                pltpu.VMEM(current.shape, F32),
+                dma((6,)),
+                dma((energies,)),
                 pltpu.VMEM((ITERS, 2, energies) + block, F32),
                 pltpu.VMEM((ITERS, 2, energies) + block, F32),
                 pltpu.VMEM((ITERS, energies) + block, F32),
@@ -337,7 +372,7 @@
                 dma((ITERS, 2, energies)),
             ],
             compiler_params=pltpu.CompilerParams(
-                collective_id=0, has_side_effects=True, vmem_limit_bytes=48 * 1024 * 1024),
+                collective_id=0, has_side_effects=True),
         )(phonon_weights, current, local_ret, coupling_on, coupling_lower, coupling_upper)
         return result[:, None]
 

time: 66 us -> 62 us (0.939)
  local copies, waits for them, and re-layouts: 6.59 us -> 2.3 us
    unnamed x13 -> x1, local copies, waits for them, and re-layouts: 6.59 us -> 2.3 us
where the time goes in v4:
time: 62 us; the launch traced here: 61.6 us
  Pallas kernels  59.3 us (96%)
  local copies, waits for them, and re-layouts  2.3 us (4%)
    pallas_call x1, Pallas kernels, local(): pl.pallas_call(functools.partial(kernel, counts), out_shape=jax.ShapeDtyp...  59.3 us
    unnamed x1, local copies, waits for them, and re-layouts  2.3 us

profile of v4, /device:TPU:5, one launch (start us, length us, event | category | flops | bytes accessed | tf_op | source)
XLA Modules:
  0.0 61.6 jit_solution(6874542365761063692)
XLA Ops:
  0.0 59.3 %shard_map.64 = f32[8,2,128,128]{3,2,1,0:T(8,128)} custom-call(f32[4]{0:T(128)} %weights_in.1, f32[8,2,128,128]{3,2,1,0:T(8,128)} %bitcast.6, f32[8,2,128,128]{3,2,1,0:T(8,128)} %bitcast.7, f32[1,128,128]{2,1,0:T(8,128)} %on_in.1, f32[1,128,128]{2,1,0:T(8,128)} %low_in.1, f32[1,128,128]{2,1,0:T(8,128)} %up_in.1), custom_call_target="tpu_custom_call" | custom-call | tf_op jit(solution)/shard_map/pallas_call | solution.py:346
  59.3 2.3 %copy.9 = f32[8,1,2,128,128]{4,3,2,1,0:T(8,128)} copy(f32[8,1,2,128,128]{4,3,2,1,0:T(8,128)} %bitcast.5) | data formatting | bytes 2097152

commit v5 on v4

--- a/solution.py
+++ b/solution.py
@@ -12,7 +12,7 @@
 ITERS = 2
 
 LAG = 2
-POLLS = 2
+POLLS = 4
 
 MESH = pl.DeviceIdType.MESH
 F32 = jnp.float32
@@ -64,7 +64,7 @@
     counts, weights_in, green_in, retarded_in, on_in, low_in, up_in, out_hbm,
     weights, green, retarded, c_on, c_low, c_up, out, load_sem, store_sem,
     halo, rim, mixed, middle, c_right, c_left, r_left, r_right,
-    e_send, e_recv, s_send, s_recv,
+    e_send, e_recv, s_send, s_recv, detour, t_send, t_recv,
 ):
     n_energy, n_slab = counts
     energies, _, size, _ = green.shape
@@ -146,12 +146,36 @@
     def source(step, e):
         return green_in.at[real(e)] if step == 0 else middle.at[step - 1, e]
 
-    def energy_copy(step, lane, src, to, side, slot):
+    def energy_copy(step, lane, src, to, side, slot, half=False):
+        dst = halo.at[step, side, slot]
+        if half:
+            src, dst = src.at[0], dst.at[0]
         return pltpu.make_async_remote_copy(
-            src_ref=src, dst_ref=halo.at[step, side, slot],
+            src_ref=src, dst_ref=dst,
             send_sem=e_send.at[step, lane, slot], recv_sem=e_recv.at[step, side, slot],
             device_id=to, device_id_type=MESH,
         )
+
+    def detour_out(step):
+        return pltpu.make_async_remote_copy(
+            src_ref=source(step, energies - 1).at[1], dst_ref=detour.at[step],
+            send_sem=t_send.at[step, 0], recv_sem=t_recv.at[step, 0],
+            device_id=y_peer, device_id_type=MESH,
+        )
+
+    def detour_on(step):
+        return pltpu.make_async_remote_copy(
+            src_ref=detour.at[step], dst_ref=halo.at[step, 1, 0, 1],
+            send_sem=t_send.at[step, 1], recv_sem=t_recv.at[step, 1],
+            device_id=x_peer, device_id_type=MESH,
+        )
+
+    def relay_detour(step):
+        if square:
+            @pl.when(is_end)
+            def _():
+                detour_out(step).wait_recv()
+                detour_on(step).start()
 
     def slab_copy(step, side, e):
         return pltpu.make_async_remote_copy(
@@ -169,7 +193,10 @@
 
             def send(lane=lane, to=to, todo=order[start:stop], side=side):
                 for e in todo:
-                    energy_copy(step, lane, source(step, e), to, side, e).start()
+                    half = square and side == 1 and e == energies - 1
+                    energy_copy(step, lane, source(step, e), to, side, e, half).start()
+                    if half:
+                        detour_out(step).start()
             if stop > start:
                 when(flag, send)
             role.sent[step, lane] = stop
@@ -183,9 +210,13 @@
         def wait():
             for slot in role.arrivals[step][side][start:upto]:
                 block = halo.at[step, side, slot]
-                energy_copy(step, 0, block, peers[0][1], side, slot).wait_recv()
+                last = energies - 1 if role.forwards else 0
+                half = square and side == 1 and slot == last
+                energy_copy(step, 0, block, peers[0][1], side, slot, half).wait_recv()
+                if half and not role.forwards:
+                    detour_on(step).wait_recv()
                 if role.forwards and role.forwards[0] == side and slot in role.forwards[2]:
-                    energy_copy(step, 1, block, role.forwards[1], 1, energies - 1 - slot).start()
+                    energy_copy(step, 1, block, role.forwards[1], 1, energies - 1 - slot, half).start()
         when(have.get(side), wait)
 
     for role in roles:
@@ -288,10 +319,14 @@
             if i < energies:
                 for role in roles:
                     when(role.when, lambda role=role: mix(role, step, role.order[step][i]))
+            if step == 0 and i == 0:
+                relay_detour(step)
             at = i - LAG
             if at < 0:
                 continue
             ahead = at - energies + POLLS + 1
+            if step < ITERS - 1 and ahead == 1:
+                relay_detour(step + 1)
             if step < ITERS - 1 and ahead > 0:
                 for role in roles:
                     if role.forwards:
@@ -319,12 +354,17 @@
                 for lane, (flag, to, orders, side) in enumerate(role.sends):
                     def wait(lane=lane, to=to, order=orders[step], side=side):
                         for e in order:
-                            energy_copy(step, lane, source(step, e), to, side, e).wait_send()
+                            half = square and side == 1 and e == energies - 1
+                            energy_copy(step, lane, source(step, e), to, side, e, half).wait_send()
+                            if half:
+                                detour_out(step).wait_send()
                     when(flag, wait)
                 if role.forwards:
                     for slot in role.forwards[2]:
                         energy_copy(
-                            step, 1, halo.at[step, 1, slot], role.forwards[1], 1, energies - 1 - slot).wait_send()
+                            step, 1, halo.at[step, 1, slot], role.forwards[1], 1, energies - 1 - slot,
+                            slot == energies - 1).wait_send()
+                    detour_on(step).wait_send()
             when(role.when, finish)
         for side in sides:
             @pl.when(has_slab[side])
@@ -370,6 +410,9 @@
                 dma((ITERS, 2, energies)),
                 dma((ITERS, 2, energies)),
                 dma((ITERS, 2, energies)),
+                pltpu.VMEM((ITERS, size, size), F32),
+                dma((ITERS, 2)),
+                dma((ITERS, 2)),
             ],
             compiler_params=pltpu.CompilerParams(
                 collective_id=0, has_side_effects=True),

time: 62 us -> 60.4 us (0.974)
  Pallas kernels: 59.3 us -> 57.9 us
    pallas_call x1, Pallas kernels: 59.3 us -> 57.9 us  [local(): pl.pallas_call(functools.partial(kernel, counts), out_shape=jax.ShapeDtyp...]
where the time goes in v5:
time: 60.4 us; the launch traced here: 60.2 us
  Pallas kernels  57.9 us (96%)
  local copies, waits for them, and re-layouts  2.3 us (4%)
    pallas_call x1, Pallas kernels, local(): pl.pallas_call(functools.partial(kernel, counts), out_shape=jax.ShapeDtyp...  57.9 us
    unnamed x1, local copies, waits for them, and re-layouts  2.3 us

profile of v5, /device:TPU:5, one launch (start us, length us, event | category | flops | bytes accessed | tf_op | source)
XLA Modules:
  0.0 60.2 jit_solution(10316267146416522837)
XLA Ops:
  0.0 57.9 %shard_map.64 = f32[8,2,128,128]{3,2,1,0:T(8,128)} custom-call(f32[4]{0:T(128)} %weights_in.1, f32[8,2,128,128]{3,2,1,0:T(8,128)} %bitcast.6, f32[8,2,128,128]{3,2,1,0:T(8,128)} %bitcast.7, f32[1,128,128]{2,1,0:T(8,128)} %on_in.1, f32[1,128,128]{2,1,0:T(8,128)} %low_in.1, f32[1,128,128]{2,1,0:T(8,128)} %up_in.1), custom_call_target="tpu_custom_call" | custom-call | tf_op jit(solution)/shard_map/pallas_call | solution.py:386
  57.9 2.3 %copy.9 = f32[8,1,2,128,128]{4,3,2,1,0:T(8,128)} copy(f32[8,1,2,128,128]{4,3,2,1,0:T(8,128)} %bitcast.5) | data formatting | bytes 2097152
